TPU v7x, 32 devices: a whole 2x2x4 slice. The times are simulated.
32 devices in a mesh: dp: 8 (over y, x, core), mp: 4 (over z).
Axes of the slice: x: 2, y: 2, z: 4, core: 2. Of those that a mesh axis runs over, the one named last changes fastest.
Arguments:
- queries: bfloat16 [2048, 2048], P('dp', 'mp'), may hold values from -24 to 24
- context_grad: bfloat16 [2048, 2048], P('dp', 'mp'), may hold values from -6 to 6
- encoder_rows: bfloat16 [7168, 4096], P('dp'), may hold values from -60 to 60
- key_weight: bfloat16 [4096, 2048], P('dp', 'mp'), may hold values from -1 to 1
- value_weight: bfloat16 [4096, 2048], P('dp', 'mp'), may hold values from -0.09375 to 0.09375
- document_lengths: int32 [8, 4], P('dp'), may hold values from 1 to 128, 256 in all within a row
- block_bin: int32 [56], P('dp'), may hold values from 0 to 7, as said below
- block_document: int32 [56], P('dp'), may hold values from 0 to 3
Outputs:
- context: bfloat16 [2048, 2048], P('dp', 'mp')
- query_grad: bfloat16 [2048, 2048], P('dp', 'mp')
- encoder_grad: bfloat16 [7168, 4096], P('dp', 'mp')
- key_weight_grad: bfloat16 [4096, 2048], P('dp', 'mp')
- value_weight_grad: bfloat16 [4096, 2048], P('dp', 'mp')
Inputs may be any that keep to these rules, and one draw needn't show every extreme that they name: `block_bin`: each index of dp holds 7 encoder blocks and sends them to 7 different bins; one bin receives a block from every index of dp.
All inputs are finite; a program needn't handle non-finite values.
Results may differ from a plain program's by a relative error of at most 0.03.
The roundings to bfloat16 on the way count: a program that leaves them out, or rounds other values in their place, can miss the bound.
Values may be sent and summed in bfloat16 or wider, within the bound.
A program may use at most 128 MiB of HBM per device.

v0:
```python
import jax
import jax.numpy as jnp
from jax import lax
from jax.sharding import PartitionSpec as P

HD = 256
BLK = 128
masked_value = -1e30


def attend_weights(scores, live_mask):
    present = jnp.any(live_mask, axis=1)[None, :, None]
    blocked = jnp.where(live_mask[None], scores, masked_value)
    highest = jnp.max(blocked, axis=2, keepdims=True)
    highest = jnp.where(present, highest, 0.0)
    raised = jnp.exp(jnp.where(live_mask[None], scores - highest, masked_value))
    totals = jnp.maximum(jnp.sum(raised, axis=2, keepdims=True), 1.0)
    return raised / totals


def token_documents(lengths, token_count):
    doc_ends = jnp.cumsum(lengths)
    positions = jnp.arange(token_count, dtype=jnp.int32)
    return jnp.sum((doc_ends[None, :] <= positions[:, None]).astype(jnp.int32), axis=1)


def per_device(
    queries,
    context_grad,
    encoder_rows,
    key_weight,
    value_weight,
    document_lengths,
    block_bin,
    block_document,
):
    bin_count = lax.axis_size("dp")
    full_key, full_value = (
        lax.all_gather(key_weight, "dp", axis=0, tiled=True),
        lax.all_gather(value_weight, "dp", axis=0, tiled=True),
    )
    head_width = full_key.shape[1]
    head_count = head_width // HD
    block_rows = BLK
    blocks_here = block_bin.shape[0]
    both_weights = jnp.concatenate([full_key, full_value], axis=1)
    projected = jnp.dot(encoder_rows, both_weights, preferred_element_type=jnp.float32).astype(
        jnp.bfloat16
    )
    route_table = (block_bin[:, None] == jnp.arange(bin_count, dtype=jnp.int32)[None, :]).astype(
        jnp.bfloat16
    )
    flat_blocks = projected.reshape(blocks_here, block_rows * 2 * head_width)
    outbound = lax.dot_general(
        route_table, flat_blocks, (((0,), (0,)), ((), ())), preferred_element_type=jnp.float32
    )
    outbound = outbound.astype(jnp.bfloat16).reshape(bin_count, block_rows, 2 * head_width)
    slot_docs = (
        lax.dot_general(
            route_table.astype(jnp.float32),
            (block_document + 1).astype(jnp.float32),
            (((0,), (0,)), ((), ())),
        )
        - 1.0
    )
    tag_rows = jnp.broadcast_to(slot_docs[:, None], (bin_count, block_rows)).astype(jnp.bfloat16)
    arrived, arrived_tags = (
        lax.all_to_all(outbound, "dp", split_axis=0, concat_axis=0, tiled=True),
        lax.all_to_all(tag_rows, "dp", split_axis=0, concat_axis=0, tiled=True),
    )
    key_slots = arrived[:, :, :head_width].reshape(bin_count * block_rows, head_count, HD)
    value_slots = arrived[:, :, head_width:].reshape(bin_count * block_rows, head_count, HD)
    token_count = queries.shape[0]
    token_docs = token_documents(document_lengths[0], token_count).astype(jnp.float32)
    live_mask = arrived_tags.reshape(-1).astype(jnp.float32)[None, :] == token_docs[:, None]
    query_heads = queries.reshape(token_count, head_count, HD)
    grad_heads = context_grad.reshape(token_count, head_count, HD)
    scaling = HD ** (-0.5)
    scores = (
        jnp.einsum("thd,shd->hts", query_heads, key_slots, preferred_element_type=jnp.float32)
        * scaling
    )
    attention = attend_weights(scores, live_mask)
    rounded = attention.astype(jnp.bfloat16)
    context = jnp.einsum(
        "hts,shd->thd", rounded, value_slots, preferred_element_type=jnp.float32
    ).astype(jnp.bfloat16)
    grad_raw = jnp.einsum(
        "thd,shd->hts", grad_heads, value_slots, preferred_element_type=jnp.float32
    )
    deltas = jnp.sum(attention * grad_raw, axis=2, keepdims=True)
    score_grad = (attention * (grad_raw - deltas) * scaling).astype(jnp.bfloat16)
    query_grad = jnp.einsum(
        "hts,shd->thd", score_grad, key_slots, preferred_element_type=jnp.float32
    ).astype(jnp.bfloat16)
    key_grad = jnp.einsum(
        "hts,thd->shd", score_grad, query_heads, preferred_element_type=jnp.float32
    ).astype(jnp.bfloat16)
    value_grad = jnp.einsum(
        "hts,thd->shd", rounded, grad_heads, preferred_element_type=jnp.float32
    ).astype(jnp.bfloat16)
    slot_grads = jnp.concatenate(
        [
            key_grad.reshape(bin_count, block_rows, head_width),
            value_grad.reshape(bin_count, block_rows, head_width),
        ],
        axis=2,
    )
    returned = lax.all_to_all(slot_grads, "dp", split_axis=0, concat_axis=0, tiled=True)
    own_grads = jnp.dot(
        route_table,
        returned.reshape(bin_count, block_rows * 2 * head_width),
        preferred_element_type=jnp.float32,
    )
    own_grads = own_grads.astype(jnp.bfloat16).reshape(encoder_rows.shape[0], 2 * head_width)
    weight_terms = lax.dot_general(
        encoder_rows, own_grads, (((0,), (0,)), ((), ())), preferred_element_type=jnp.float32
    )
    weight_sums = lax.psum_scatter(
        weight_terms.astype(jnp.bfloat16), "dp", scatter_dimension=0, tiled=True
    ).astype(jnp.float32)
    key_weight_grad = weight_sums[:, :head_width].astype(jnp.bfloat16)
    value_weight_grad = weight_sums[:, head_width:].astype(jnp.bfloat16)
    row_terms = lax.dot_general(
        own_grads, both_weights, (((1,), (1,)), ((), ())), preferred_element_type=jnp.float32
    )
    encoder_grad = lax.psum_scatter(
        row_terms.astype(jnp.bfloat16), "mp", scatter_dimension=1, tiled=True
    )
    return (
        context.reshape(token_count, head_width),
        query_grad.reshape(token_count, head_width),
        encoder_grad,
        key_weight_grad,
        value_weight_grad,
    )


def solution(mesh):
    in_specs = (
        P("dp", "mp"),
        P("dp", "mp"),
        P("dp", None),
        P("dp", "mp"),
        P("dp", "mp"),
        P("dp", None),
        P("dp"),
        P("dp"),
    )
    out_specs = (P("dp", "mp"), P("dp", "mp"), P("dp", "mp"), P("dp", "mp"), P("dp", "mp"))
    return jax.shard_map(
        per_device, mesh=mesh, in_specs=in_specs, out_specs=out_specs, check_vma=False
    )
```

profile of v0, /device:TPU:0, one launch (start us, length us, event | category | flops | bytes accessed | tf_op | source)
XLA Modules:
  0.0 427.2 jit_solution(468431480410873868)
XLA Ops:
  7.2 0.7 all-gather.3.cloned.1.call-update
  7.9 0.7 all-gather.5.cloned.1.call-update
  8.6 0.9 fusion.12
  9.5 0.7 broadcast_in_dim.30
  10.2 5.2 %all-to-all-start.1 = ((bf16[8,1,128]{2,1,0:T(2,128)(2,1)}), bf16[8,1,128]{2,1,0:T(2,128)(2,1)S(1)}, u32[]{:S(2)}, u32[]{:S(2)}) async-start(bf16[8,1,128]{2,1,0:T(2,128)(2,1)} %broadcast_in_dim.30), calls=%async_computation.1 | async-start | bytes 8192 | tf_op jit(solution)/shard_map/all_to_all | solution.py:69
  15.4 33.8 %all-gather.3.cloned.1.call-done = bf16[4096,512]{1,0:T(8,128)(2,1)} async-done(((bf16[512,512]{1,0:T(8,128)(2,1)}), bf16[4096,512]{1,0:T(8,128)(2,1)}) %all-gather.3.cloned.1.call-update) | async-done | bytes 4194320 | tf_op jit(solution)/shard_map/all_gather | solution.py:39
  49.2 4.5 %constant_dynamic-update-slice_fusion.1 = bf16[4096,1024]{1,0:T(8,128)(2,1)} fusion(bf16[4096,512]{1,0:T(8,128)(2,1)} %all-gather.3.cloned.1.call-done), kind=kLoop, calls=%fused_computation.43 | loop fusion | bytes 8388608
  53.7 34.0 %all-gather.5.cloned.1.call-done = bf16[4096,512]{1,0:T(8,128)(2,1)} async-done(((bf16[512,512]{1,0:T(8,128)(2,1)}), bf16[4096,512]{1,0:T(8,128)(2,1)}) %all-gather.5.cloned.1.call-update) | async-done | bytes 4194320 | tf_op jit(solution)/shard_map/all_gather | solution.py:40
  87.7 4.5 %constant_dynamic-update-slice_fusion = bf16[4096,1024]{1,0:T(8,128)(2,1)} fusion(bf16[4096,1024]{1,0:T(8,128)(2,1)} %constant_dynamic-update-slice_fusion.1, bf16[4096,512]{1,0:T(8,128)(2,1)} %all-gather.5.cloned.1.call-done), kind=kLoop, calls=%fused_computation.42 | loop fusion | bytes 8388608 | tf_op jit(solution)/shard_map/concatenate | solution.py:46
  92.2 13.4 %convert_bitcast_fusion.1 = bf16[896,1024]{0,1:T(8,128)(2,1)S(1)} fusion(bf16[4096,1024]{1,0:T(8,128)(2,1)} %constant_dynamic-update-slice_fusion, bf16[896,4096]{1,0:T(8,128)(2,1)} %param.10), kind=kOutput, calls=%fused_computation.16 | convolution fusion | flops 7517110272 | bytes 17563648 | tf_op jit(solution)/shard_map/dot_general | solution.py:47
  105.6 2.4 copy.79
  108.0 3.8 reshape.137
  111.8 2.2 convolution_convert_fusion.1
  114.0 4.1 copy.80
  118.2 3.7 all-to-all-start
  122.7 25.8 %all-to-all-done = bf16[8,128,1024]{1,2,0:T(8,128)(2,1)S(1)} async-done(((bf16[8,128,1024]{1,2,0:T(8,128)(2,1)}), bf16[8,128,1024]{1,2,0:T(8,128)(2,1)S(1)}, u32[]{:S(2)}, u32[]{:S(2)}) %all-to-all-start) | async-done | bytes 2097184 | tf_op jit(solution)/shard_map/all_to_all | solution.py:68
  148.5 1.1 fusion.43
  149.6 0.7 copy.81
  150.3 0.5 reshape.139
  150.8 0.7 copy.82
  151.5 0.5 reshape.142
  152.0 1.8 fusion.4
  153.8 0.5 fusion.8
  154.3 0.6 copy-done.5
  154.9 1.9 fusion.17
  156.8 0.7 fusion.10
  157.5 0.5 copy.92
  158.4 6.1 %fusion.9 = bf16[1024,2,256]{2,0,1:T(8,128)(2,1)} fusion(f32[2,1024,256]{2,1,0:T(8,128)} %fusion.17, bf16[32,2,8,256]{3,2,1,0:T(8,128)(2,1)} %bitcast.136, f32[2,1024,256]{2,1,0:T(8,128)} %copy-done.1, f32[2,256]{1,0:T(2,128)S(1)} %broadcast_maximum_fusion, f32[2,256]{1,0:T(2,128)S(1)} %broadcast_select_fusion, pred[256,1024]{0,1:T(8,128)(4,1)S(1)} %get-tuple-element.35), kind=kOutput, calls=%fused_computation.21 | convolution fusion | flops 275777024 | bytes 5771264 | tf_op jit(solution)/shard_map/hts,thd->shd/dot_general | solution.py:96
  164.5 1.5 copy.90
  166.7 29.0 %all_to_all.16 = bf16[8,128,1024]{1,2,0:T(8,128)(2,1)S(1)} all-to-all(bf16[8,128,1024]{1,2,0:T(8,128)(2,1)S(1)} %copy.93), channel_id=1, replica_groups=mesh['dp'=8,'mp'=4] {'dp'}, dimensions={0} | all-to-all | bytes 4194304 | tf_op jit(solution)/shard_map/all_to_all | solution.py:109
  195.7 2.6 copy.94
  198.4 2.7 copy.107
  201.1 0.8 convolution_convert_fusion
  201.9 4.0 reshape.150
  205.8 13.8 %convert_bitcast_fusion = bf16[4096,1024]{0,1:T(8,128)(2,1)} fusion(bf16[896,1024]{1,0:T(8,128)(2,1)} %reshape.150, bf16[896,4096]{1,0:T(8,128)(2,1)} %param.10), kind=kOutput, calls=%fused_computation.3 | convolution fusion | flops 7520387072 | bytes 17563648 | tf_op jit(solution)/shard_map/dot_general | solution.py:116
  219.6 0.3 reduce-scatter.3.cloned.1.call-start
  219.9 1.2 copy-done.3
  221.1 13.4 %convolution_convert_fusion.2 = bf16[896,4096]{1,0:T(8,128)(2,1)} fusion(bf16[896,1024]{1,0:T(8,128)(2,1)S(1)} %copy-done.3, bf16[4096,1024]{1,0:T(8,128)(2,1)} %constant_dynamic-update-slice_fusion), kind=kOutput, calls=%fused_computation.4 | convolution fusion | flops 7519862784 | bytes 17563648 | tf_op jit(solution)/shard_map/dot_general | solution.py:124
  234.5 1.7 copy-done.2
  236.2 1.5 convolution_convert_fusion.6
  237.7 1.8 copy.95
  239.5 4.2 convolution_convert_fusion.5
  243.7 0.8 copy.96
  244.5 45.7 %reduce-scatter.5.cloned.1.call-done = bf16[512,1024]{0,1:T(8,128)(2,1)} async-done(((bf16[4096,1024]{0,1:T(8,128)(2,1)}), bf16[512,1024]{0,1:T(8,128)(2,1)}) %reduce-scatter.5.cloned.1.call-update) | async-done | bytes 1048592 | tf_op jit(solution)/shard_map/reduce_scatter | solution.py:119
  290.2 1.3 fusion.44
  291.4 1.0 copy.97
  292.4 1.0 copy.98
  293.5 127.3 %reduce-scatter.3.cloned.1.call-done = bf16[896,1024]{1,0:T(8,128)(2,1)} async-done(((bf16[896,4096]{1,0:T(8,128)(2,1)}), bf16[896,1024]{1,0:T(8,128)(2,1)}) %reduce-scatter.3.cloned.1.call-update) | async-done | bytes 1835024 | tf_op jit(solution)/shard_map/reduce_scatter | solution.py:127
  (30 shorter events, 1.9 us)
Async XLA Ops:
  7.2 42.0 %all-gather.3.cloned.1.call-start = ((), (), s32[]{:S(2)}) async-start(), calls=%async_computation.5 | async-start | bytes 4718592 | tf_op jit(solution)/shard_map/all_gather | solution.py:39
  7.9 79.8 %all-gather.5.cloned.1.call-start = ((), (), s32[]{:S(2)}) async-start(), calls=%async_computation.6 | async-start | bytes 4718592 | tf_op jit(solution)/shard_map/all_gather | solution.py:40
  10.2 108.0 %all-to-all-start.1 = ((bf16[8,1,128]{2,1,0:T(2,128)(2,1)}), bf16[8,1,128]{2,1,0:T(2,128)(2,1)S(1)}, u32[]{:S(2)}, u32[]{:S(2)}) async-start(bf16[8,1,128]{2,1,0:T(2,128)(2,1)} %broadcast_in_dim.30), calls=%async_computation.1 | async-start | bytes 8192 | tf_op jit(solution)/shard_map/all_to_all | solution.py:69
  108.0 3.8 copy-start.6
  118.2 4.0 copy-start.7
  118.2 30.3 %all-to-all-start = ((bf16[8,128,1024]{1,2,0:T(8,128)(2,1)}), bf16[8,128,1024]{1,2,0:T(8,128)(2,1)S(1)}, u32[]{:S(2)}, u32[]{:S(2)}) async-start(bf16[8,128,1024]{1,2,0:T(8,128)(2,1)} %copy.80), calls=%async_computation | async-start | bytes 4194304 | tf_op jit(solution)/shard_map/all_to_all | solution.py:68
  121.9 168.3 %reduce-scatter.5.cloned.1.call-start = ((), (), s32[]{:S(2)}) async-start(), calls=%async_computation.8 | async-start | bytes 9437184 | tf_op jit(solution)/shard_map/reduce_scatter | solution.py:119
  149.6 1.2 copy-start
  152.0 2.3 copy-start.4
  153.8 3.1 copy-start.1
  153.8 1.1 copy-start.5
  219.6 1.5 copy-start.3
  219.6 201.1 %reduce-scatter.3.cloned.1.call-start = ((), (), s32[]{:S(2)}) async-start(), calls=%async_computation.7 | async-start | bytes 9175040 | tf_op jit(solution)/shard_map/reduce_scatter | solution.py:127
  234.5 1.7 copy-start.2
Sparse Core Ops, SparseCore 0:
  9.9 39.2 all-gather.2
  51.1 36.5 all-gather.4
  219.7 70.3 reduce-scatter.4
  292.9 127.7 reduce-scatter.2
where the time goes:
time: 428 us; the launch traced here: 427 us
  waiting for transfers between devices  268 us (63%)
  matrix products  60.6 us (14%)
  local copies, waits for them, and re-layouts  44.9 us (10%)
  blocking collectives  29 us (7%)
  between operations  14 us (3%)
  starting transfers between devices  9.53 us (2%)
    reduce_scatter x1, waiting for transfers between devices, per_device(): lax.psum_scatter(row_terms.astype(jnp.bfloat16), 'mp', scatter_dimension=...  127 us
    reduce_scatter x1, waiting for transfers between devices, per_device(): lax.psum_scatter(weight_terms.astype(jnp.bfloat16), 'dp', scatter_dimensi...  45.7 us
    all_gather x1, waiting for transfers between devices, per_device(): lax.all_gather(value_weight, 'dp', axis=0, tiled=True)  34 us
    all_gather x1, waiting for transfers between devices, per_device(): lax.all_gather(key_weight, 'dp', axis=0, tiled=True)  33.8 us
    all_to_all x1, blocking collectives, per_device(): lax.all_to_all(slot_grads, 'dp', split_axis=0, concat_axis=0, tiled=True)  29 us
    all_to_all x1, waiting for transfers between devices, per_device(): lax.all_to_all(outbound, 'dp', split_axis=0, concat_axis=0, tiled=True)  25.8 us
    unnamed x24, local copies, waits for them, and re-layouts  15.9 us
    dot_general x1, matrix products, per_device(): lax.dot_general(encoder_rows, own_grads, (((0,), (0,)), ((), ())), prefer...  13.8 us
  transfers between devices with their start and end apart: 6, of which 5 were waited for; matrix products, arithmetic and copies ran while one was open for 15% of the time, Pallas kernels for 0%

commit v1 on v0

--- a/solution.py
+++ b/solution.py
@@ -6,6 +6,19 @@
 HD = 256
 BLK = 128
 masked_value = -1e30
+
+
+def collect(x, axis, dim):
+    ways = lax.axis_size(axis)
+    up = [(d, (d + 1) % ways) for d in range(ways)]
+    down = [(d, (d - 1) % ways) for d in range(ways)]
+    earlier, later = ([x], [x])
+    for _ in range(ways // 2):
+        earlier.append(lax.ppermute(earlier[-1], axis, up))
+    for _ in range((ways - 1) // 2):
+        later.append(lax.ppermute(later[-1], axis, down))
+    line = jnp.concatenate([*earlier[::-1], *later[1:]], axis=dim)
+    return jnp.roll(line, (lax.axis_index(axis) - ways // 2) * x.shape[dim], axis=dim)
 
 
 def attend_weights(scores, live_mask):
@@ -36,7 +49,7 @@
 ):
     bin_count = lax.axis_size("dp")
     full_key, full_value = (
-        lax.all_gather(key_weight, "dp", axis=0, tiled=True),
+        collect(key_weight, "dp", 0),
         lax.all_gather(value_weight, "dp", axis=0, tiled=True),
     )
     head_width = full_key.shape[1]

time: 428 us -> 419 us (0.979)
  waiting for transfers between devices: 268 us -> 254 us
  starting transfers between devices: 9.53 us -> 20.6 us
  local copies, waits for them, and re-layouts: 44.9 us -> 38.9 us
    ppermute x0 -> x7, waiting for transfers between devices: none -> 53.4 us  [the longest x4 47 us: collect(): earlier.append(lax.ppermute(earlier[-1], axis, up))]
    all_gather x1, waiting for transfers between devices: 34 us -> 0.01 us  [per_device(): lax.all_gather(value_weight, 'dp', axis=0, tiled=True)]
    all_gather x1 -> x0, waiting for transfers between devices: 33.8 us -> none  [per_device(): lax.all_gather(key_weight, 'dp', axis=0, tiled=True)]
    ppermute x0 -> x7, starting transfers between devices: none -> 8.53 us  [the longest x3 7.97 us: collect(): later.append(lax.ppermute(later[-1], axis, down))]
    concatenate x1, local copies, waits for them, and re-layouts: 4.46 us -> 0.04 us  [collect(): jnp.roll(line, (lax.axis_index(axis) - ways // 2) * x.shape[dim], axis=dim)]
    unnamed x24 -> x40, local copies, waits for them, and re-layouts: 15.9 us -> 12 us
  transfers between devices with their start and end apart: 6 -> 12, of which waited for: 5 -> 7; matrix products, arithmetic and copies ran while one was open for 15% -> 13% of each run, Pallas kernels for 0% -> 0%
where the time goes in v1:
time: 419 us
  waiting for transfers between devices  254 us (61%)
  matrix products  60.9 us (15%)
  local copies, waits for them, and re-layouts  38.9 us (9%)
  blocking collectives  29 us (7%)
  starting transfers between devices  20.6 us (5%)
  between operations  14.1 us (3%)
    reduce_scatter x1, waiting for transfers between devices, per_device(): lax.psum_scatter(row_terms.astype(jnp.bfloat16), 'mp', scatter_dimension=...  127 us
    ppermute x4, waiting for transfers between devices, collect(): earlier.append(lax.ppermute(earlier[-1], axis, up))  47 us
    reduce_scatter x1, waiting for transfers between devices, per_device(): lax.psum_scatter(weight_terms.astype(jnp.bfloat16), 'dp', scatter_dimensi...  46.5 us
    all_to_all x1, blocking collectives, per_device(): lax.all_to_all(slot_grads, 'dp', split_axis=0, concat_axis=0, tiled=True)  29 us
    all_to_all x1, waiting for transfers between devices, per_device(): lax.all_to_all(outbound, 'dp', split_axis=0, concat_axis=0, tiled=True)  25.8 us
    dot_general x1, matrix products, per_device(): lax.dot_general(encoder_rows, own_grads, (((0,), (0,)), ((), ())), prefer...  13.9 us
    dot_general x1, matrix products, per_device(): lax.dot_general(own_grads, both_weights, (((1,), (1,)), ((), ())), prefer...  13.5 us
    dot_general x1, matrix products, per_device(): jnp.dot(encoder_rows, both_weights, preferred_element_type=jnp.float32)  13.5 us
  transfers between devices with their start and end apart: 12, of which 7 were waited for; matrix products, arithmetic and copies ran while one was open for 13% of the time, Pallas kernels for 0%

profile of v1, /device:TPU:0, one launch (start us, length us, event | category | flops | bytes accessed | tf_op | source)
XLA Modules:
  0.0 418.6 jit_solution(10139530978027451725)
XLA Ops:
  7.2 0.7 all-gather.2.cloned.1.call-update
  7.9 0.5 collective-permute-start
  8.4 9.9 %collective-permute-done = bf16[512,512]{1,0:T(8,128)(2,1)S(1)} collective-permute-done((bf16[512,512]{1,0:T(8,128)(2,1)}, bf16[512,512]{1,0:T(8,128)(2,1)S(1)}, u32[]{:S(2)}, u32[]{:S(2)}) %collective-permute-start) | collective-permute-done | bytes 524320 | tf_op jit(solution)/shard_map/ppermute | solution.py:17
  18.4 2.6 collective-permute-start.4
  21.0 16.5 %collective-permute-done.1 = bf16[512,512]{1,0:T(8,128)(2,1)S(1)} collective-permute-done((bf16[512,512]{1,0:T(8,128)(2,1)S(1)}, bf16[512,512]{1,0:T(8,128)(2,1)S(1)}, u32[]{:S(2)}, u32[]{:S(2)}) %collective-permute-start.1) | collective-permute-done | bytes 524320 | tf_op jit(solution)/shard_map/ppermute | solution.py:17
  37.6 2.6 collective-permute-start.5
  40.2 20.5 %collective-permute-done.2 = bf16[512,512]{1,0:T(8,128)(2,1)S(1)} collective-permute-done((bf16[512,512]{1,0:T(8,128)(2,1)S(1)}, bf16[512,512]{1,0:T(8,128)(2,1)S(1)}, u32[]{:S(2)}, u32[]{:S(2)}) %collective-permute-start.2) | collective-permute-done | bytes 524320 | tf_op jit(solution)/shard_map/ppermute | solution.py:17
  60.8 0.9 fusion.13
  61.6 0.7 broadcast_in_dim.30
  62.3 7.3 %all-to-all-start.1 = ((bf16[8,1,128]{2,1,0:T(2,128)(2,1)}), bf16[8,1,128]{2,1,0:T(2,128)(2,1)S(1)}, u32[]{:S(2)}, u32[]{:S(2)}) async-start(bf16[8,1,128]{2,1,0:T(2,128)(2,1)} %broadcast_in_dim.30), calls=%async_computation.1 | async-start | bytes 8192 | tf_op jit(solution)/shard_map/all_to_all | solution.py:82
  69.6 2.7 collective-permute-start.6
  72.7 6.4 %collective-permute-done.6 = bf16[512,512]{1,0:T(8,128)(2,1)S(1)} collective-permute-done((bf16[512,512]{1,0:T(8,128)(2,1)S(1)}, bf16[512,512]{1,0:T(8,128)(2,1)S(1)}, u32[]{:S(2)}, u32[]{:S(2)}) %collective-permute-start.6) | collective-permute-done | bytes 524320 | tf_op jit(solution)/shard_map/ppermute | solution.py:19
  79.4 2.3 constant_dynamic-slice_fusion
  81.7 13.5 %convert_bitcast_fusion.1 = bf16[896,1024]{0,1:T(8,128)(2,1)S(1)} fusion(bf16[896,4096]{1,0:T(8,128)(2,1)} %param.10, bf16[4096,512]{1,0:T(8,128)(2,1)} %all-gather.2.cloned.1.call-done, bf16[4096,512]{1,0:T(8,128)(2,1)} %constant_dynamic-slice_fusion), kind=kOutput, calls=%fused_computation.18 | convolution fusion | flops 7533887488 | bytes 17563648 | tf_op jit(solution)/shard_map/dot_general | solution.py:60
  95.2 2.4 copy.79
  97.6 3.8 reshape.137
  101.4 2.2 convolution_convert_fusion.1
  103.6 4.1 copy.80
  107.8 4.2 %all-to-all-start = ((bf16[8,128,1024]{1,2,0:T(8,128)(2,1)}), bf16[8,128,1024]{1,2,0:T(8,128)(2,1)S(1)}, u32[]{:S(2)}, u32[]{:S(2)}) async-start(bf16[8,128,1024]{1,2,0:T(8,128)(2,1)} %copy.80), calls=%async_computation | async-start | bytes 4194304 | tf_op jit(solution)/shard_map/all_to_all | solution.py:81
  112.7 25.8 %all-to-all-done = bf16[8,128,1024]{1,2,0:T(8,128)(2,1)S(1)} async-done(((bf16[8,128,1024]{1,2,0:T(8,128)(2,1)}), bf16[8,128,1024]{1,2,0:T(8,128)(2,1)S(1)}, u32[]{:S(2)}, u32[]{:S(2)}) %all-to-all-start) | async-done | bytes 2097184 | tf_op jit(solution)/shard_map/all_to_all | solution.py:81
  138.6 1.1 fusion.46
  139.7 0.7 copy.81
  140.9 0.7 copy.82
  142.1 1.8 fusion.5
  144.4 0.6 copy-done.6
  145.0 1.9 fusion.18
  147.0 0.7 fusion.11
  147.7 0.5 copy.92
  148.5 6.2 %fusion.10 = bf16[1024,2,256]{2,0,1:T(8,128)(2,1)} fusion(f32[2,1024,256]{2,1,0:T(8,128)} %fusion.18, bf16[32,2,8,256]{3,2,1,0:T(8,128)(2,1)} %bitcast.134, f32[2,1024,256]{2,1,0:T(8,128)} %copy-done.1, f32[2,256]{1,0:T(2,128)S(1)} %broadcast_maximum_fusion, f32[2,256]{1,0:T(2,128)S(1)} %broadcast_select_fusion, pred[256,1024]{0,1:T(8,128)(4,1)S(1)} %get-tuple-element.35), kind=kOutput, calls=%fused_computation.23 | convolution fusion | flops 275777024 | bytes 5771264 | tf_op jit(solution)/shard_map/hts,thd->shd/dot_general | solution.py:109
  154.7 1.5 copy.90
  156.9 29.0 %all_to_all.16 = bf16[8,128,1024]{1,2,0:T(8,128)(2,1)S(1)} all-to-all(bf16[8,128,1024]{1,2,0:T(8,128)(2,1)S(1)} %copy.93), channel_id=1, replica_groups=mesh['dp'=8,'mp'=4] {'dp'}, dimensions={0} | all-to-all | bytes 4194304 | tf_op jit(solution)/shard_map/all_to_all | solution.py:122
  185.9 2.6 copy.94
  188.5 2.7 copy.107
  191.3 0.8 convolution_convert_fusion
  192.0 4.0 reshape.150
  196.0 13.9 %convert_bitcast_fusion = bf16[4096,1024]{0,1:T(8,128)(2,1)} fusion(bf16[896,1024]{1,0:T(8,128)(2,1)} %reshape.150, bf16[896,4096]{1,0:T(8,128)(2,1)} %param.10), kind=kOutput, calls=%fused_computation.4 | convolution fusion | flops 7520387072 | bytes 17563648 | tf_op jit(solution)/shard_map/dot_general | solution.py:129
  210.2 1.2 copy-done.4
  211.4 13.5 %convolution_convert_fusion.2 = bf16[896,4096]{1,0:T(8,128)(2,1)} fusion(bf16[896,1024]{1,0:T(8,128)(2,1)S(1)} %copy-done.4, bf16[4096,512]{1,0:T(8,128)(2,1)} %all-gather.2.cloned.1.call-done, bf16[4096,512]{1,0:T(8,128)(2,1)} %constant_dynamic-slice_fusion), kind=kOutput, calls=%fused_computation.5 | convolution fusion | flops 7536640000 | bytes 17563648 | tf_op jit(solution)/shard_map/dot_general | solution.py:137
  224.9 1.7 copy-done.2
  226.6 1.5 convolution_convert_fusion.6
  228.0 1.8 copy.95
  229.8 4.2 %convolution_convert_fusion.5 = bf16[2,256,256]{2,1,0:T(8,128)(2,1)S(1)} fusion(bf16[1024,2,256]{0,2,1:T(8,128)(2,1)} %copy-done.5, f32[2,1024,256]{2,1,0:T(8,128)} %fusion.18, f32[2,1024,256]{2,1,0:T(8,128)S(1)} %copy-done.2, f32[2,256]{1,0:T(2,128)S(1)} %broadcast_maximum_fusion, f32[2,256]{1,0:T(2,128)S(1)} %broadcast_select_fusion, ...), kind=kOutput, calls=%fused_computation.25 | convolution fusion | flops 275383808 | bytes 5771264 | tf_op jit(solution)/shard_map/hts,shd->thd/dot_general | solution.py:106
  234.0 0.8 copy.96
  234.9 46.5 %reduce-scatter.5.cloned.1.call-done = bf16[512,1024]{0,1:T(8,128)(2,1)} async-done(((bf16[4096,1024]{0,1:T(8,128)(2,1)}), bf16[512,1024]{0,1:T(8,128)(2,1)}) %reduce-scatter.5.cloned.1.call-update) | async-done | bytes 1048592 | tf_op jit(solution)/shard_map/reduce_scatter | solution.py:132
  281.4 1.3 fusion.47
  282.6 1.0 copy.97
  283.6 1.0 copy.98
  284.6 127.4 %reduce-scatter.3.cloned.1.call-done = bf16[896,1024]{1,0:T(8,128)(2,1)} async-done(((bf16[896,4096]{1,0:T(8,128)(2,1)}), bf16[896,1024]{1,0:T(8,128)(2,1)}) %reduce-scatter.3.cloned.1.call-update) | async-done | bytes 1835024 | tf_op jit(solution)/shard_map/reduce_scatter | solution.py:140
  (58 shorter events, 4.3 us)
Async XLA Ops:
  7.2 74.5 %all-gather.2.cloned.1.call-start = ((), (), s32[]{:S(2)}) async-start(), calls=%async_computation.5 | async-start | bytes 4718592 | tf_op jit(solution)/shard_map/all_gather | solution.py:53
  7.9 10.5 %collective-permute-start = (bf16[512,512]{1,0:T(8,128)(2,1)}, bf16[512,512]{1,0:T(8,128)(2,1)S(1)}, u32[]{:S(2)}, u32[]{:S(2)}) collective-permute-start(bf16[512,512]{1,0:T(8,128)(2,1)} %param.11), channel_id=1, source_target_pairs={{0,4},{4,8},{8,12},{12,16},{16,20},{20,24},{24,28},{28,0},{1,5},{5... | collective-permute-start | bytes 1572872 | tf_op jit(solution)/shard_map/ppermute | solution.py:17
  18.4 19.2 %collective-permute-start.1 = (bf16[512,512]{1,0:T(8,128)(2,1)S(1)}, bf16[512,512]{1,0:T(8,128)(2,1)S(1)}, u32[]{:S(2)}, u32[]{:S(2)}) collective-permute-start(bf16[512,512]{1,0:T(8,128)(2,1)S(1)} %collective-permute-done), channel_id=1, source_target_pairs={{0,4},{4,8},{8,12},{12,16},{16,20},{20,24},{24,28},{28,0},{1,5},{5... | collective-permute-start | bytes 1572872 | tf_op jit(solution)/shard_map/ppermute | solution.py:17
  18.4 19.2 %collective-permute-start.4 = (bf16[512,512]{1,0:T(8,128)(2,1)}, bf16[512,512]{1,0:T(8,128)(2,1)S(1)}, u32[]{:S(2)}, u32[]{:S(2)}) collective-permute-start(bf16[512,512]{1,0:T(8,128)(2,1)} %param.11), channel_id=1, source_target_pairs={{0,28},{4,0},{8,4},{12,8},{16,12},{20,16},{24,20},{28,24},{1,29},{... | collective-permute-start | bytes 1572872 | tf_op jit(solution)/shard_map/ppermute | solution.py:19
  37.6 23.2 %collective-permute-start.2 = (bf16[512,512]{1,0:T(8,128)(2,1)S(1)}, bf16[512,512]{1,0:T(8,128)(2,1)S(1)}, u32[]{:S(2)}, u32[]{:S(2)}) collective-permute-start(bf16[512,512]{1,0:T(8,128)(2,1)S(1)} %collective-permute-done.1), channel_id=1, source_target_pairs={{0,4},{4,8},{8,12},{12,16},{16,20},{20,24},{24,28},{28,0},{1,5},{5... | collective-permute-start | bytes 1572872 | tf_op jit(solution)/shard_map/ppermute | solution.py:17
  37.6 32.1 %collective-permute-start.5 = (bf16[512,512]{1,0:T(8,128)(2,1)S(1)}, bf16[512,512]{1,0:T(8,128)(2,1)S(1)}, u32[]{:S(2)}, u32[]{:S(2)}) collective-permute-start(bf16[512,512]{1,0:T(8,128)(2,1)S(1)} %collective-permute-done.4), channel_id=1, source_target_pairs={{0,28},{4,0},{8,4},{12,8},{16,12},{20,16},{24,20},{28,24},{1,29},{... | collective-permute-start | bytes 1572872 | tf_op jit(solution)/shard_map/ppermute | solution.py:19
  60.8 11.6 %collective-permute-start.3 = (bf16[512,512]{1,0:T(8,128)(2,1)S(1)}, bf16[512,512]{1,0:T(8,128)(2,1)S(1)}, u32[]{:S(2)}, u32[]{:S(2)}) collective-permute-start(bf16[512,512]{1,0:T(8,128)(2,1)S(1)} %collective-permute-done.2), channel_id=1, source_target_pairs={{0,4},{4,8},{8,12},{12,16},{16,20},{20,24},{24,28},{28,0},{1,5},{5... | collective-permute-start | bytes 1572872 | tf_op jit(solution)/shard_map/ppermute | solution.py:17
  62.3 45.4 %all-to-all-start.1 = ((bf16[8,1,128]{2,1,0:T(2,128)(2,1)}), bf16[8,1,128]{2,1,0:T(2,128)(2,1)S(1)}, u32[]{:S(2)}, u32[]{:S(2)}) async-start(bf16[8,1,128]{2,1,0:T(2,128)(2,1)} %broadcast_in_dim.30), calls=%async_computation.1 | async-start | bytes 8192 | tf_op jit(solution)/shard_map/all_to_all | solution.py:82
  69.6 2.9 copy-start.3
  69.6 9.4 %collective-permute-start.6 = (bf16[512,512]{1,0:T(8,128)(2,1)S(1)}, bf16[512,512]{1,0:T(8,128)(2,1)S(1)}, u32[]{:S(2)}, u32[]{:S(2)}) collective-permute-start(bf16[512,512]{1,0:T(8,128)(2,1)S(1)} %collective-permute-done.5), channel_id=1, source_target_pairs={{0,28},{4,0},{8,4},{12,8},{16,12},{20,16},{24,20},{28,24},{1,29},{... | collective-permute-start | bytes 1572872 | tf_op jit(solution)/shard_map/ppermute | solution.py:19
  97.6 3.8 copy-start.7
  107.7 4.5 %copy-start.8 = (s32[1,4]{1,0:T(1,128)S(1)}, s32[1,4]{1,0:T(1,128)}, u32[]{:S(2)}) copy-start(s32[1,4]{1,0:T(1,128)} %param.13) | copy-start | bytes 52
  107.8 30.8 %all-to-all-start = ((bf16[8,128,1024]{1,2,0:T(8,128)(2,1)}), bf16[8,128,1024]{1,2,0:T(8,128)(2,1)S(1)}, u32[]{:S(2)}, u32[]{:S(2)}) async-start(bf16[8,128,1024]{1,2,0:T(8,128)(2,1)} %copy.80), calls=%async_computation | async-start | bytes 4194304 | tf_op jit(solution)/shard_map/all_to_all | solution.py:81
  112.0 169.4 %reduce-scatter.5.cloned.1.call-start = ((), (), s32[]{:S(2)}) async-start(), calls=%async_computation.7 | async-start | bytes 9437184 | tf_op jit(solution)/shard_map/reduce_scatter | solution.py:132
  139.7 1.2 copy-start
  142.1 2.3 copy-start.5
  143.9 3.1 copy-start.1
  143.9 1.1 copy-start.6
  209.9 1.5 copy-start.4
  209.9 202.1 %reduce-scatter.3.cloned.1.call-start = ((), (), s32[]{:S(2)}) async-start(), calls=%async_computation.6 | async-start | bytes 9175040 | tf_op jit(solution)/shard_map/reduce_scatter | solution.py:140
  224.9 1.7 copy-start.2
Sparse Core Ops, SparseCore 0:
  9.9 55.0 all-gather.1
  210.0 71.2 reduce-scatter.4
  284.2 127.7 reduce-scatter.2
